TPU v7x, 32 devices: a whole 2x2x4 slice. The times are simulated.
32 devices in a mesh: dp: 8 (over y, x, core), blk: 4 (over z).
Axes of the slice: x: 2, y: 2, z: 4, core: 2. Of those that a mesh axis runs over, the one named last changes fastest.
Arguments:
- tokens: bfloat16 [24, 1024, 1024], P('dp', 'blk'), may hold values from -6 to 6
- cotangent: bfloat16 [24, 1024, 1024], P('dp', 'blk'), may hold values from -6 to 6
- domain_ids: int32 [24, 1024], P('dp', 'blk'), may hold values from 0 to 21
- domain_weight: float32 [22], replicated, may hold values from 0.3 to 3
- frozen_input_weights: bfloat16 [1024, 8192], P('dp'), may hold values from -0.1875 to 0.1875
- bias_in: bfloat16 [8192], replicated, may hold values from -1.25 to 1.25
- frozen_down_weight: bfloat16 [4096, 1024], P('dp'), may hold values from -0.09375 to 0.09375
- bias_ff: bfloat16 [1024], replicated, may hold values from -1.25 to 1.25
- norm_gain: float32 [2, 1024], replicated, may hold values from 0.5 to 1.5
- norm_shift: float32 [2, 1024], replicated, may hold values from -1.25 to 1.25
- adapt_a: float32 [1024, 384], P('dp'), may hold values from -0.1875 to 0.1875
- adapt_a_ff: float32 [4096, 128], P('dp'), may hold values from -0.09375 to 0.09375
- adapt_b: float32 [128, 8192], P(None, 'dp'), may hold values from -0.5 to 0.5
- adapt_b_ff: float32 [128, 1024], P(None, 'dp'), may hold values from -0.5 to 0.5
- mean_a: float32 [1024, 384], P('dp'), may hold values from -192 to 192
- mean_a_ff: float32 [4096, 128], P('dp'), may hold values from -192 to 192
- mean_b: float32 [128, 8192], P(None, 'dp'), may hold values from -192 to 192
- mean_b_ff: float32 [128, 1024], P(None, 'dp'), may hold values from -192 to 192
- square_a: float32 [1024, 384], P('dp'), may hold values from 100 to 100000
- square_a_ff: float32 [4096, 128], P('dp'), may hold values from 100 to 100000
- square_b: float32 [128, 8192], P(None, 'dp'), may hold values from 100 to 100000
- square_b_ff: float32 [128, 1024], P(None, 'dp'), may hold values from 100 to 100000
- keep_a: int32 [1024, 384], P('dp'), may hold values 0 or 1
- keep_a_ff: int32 [4096, 128], P('dp'), may hold values 0 or 1
- keep_b: int32 [128, 8192], P(None, 'dp'), may hold values 0 or 1
- keep_b_ff: int32 [128, 1024], P(None, 'dp'), may hold values 0 or 1
Outputs:
- mixed: bfloat16 [24, 1024, 1024], P('dp', 'blk')
- grad_tokens: bfloat16 [24, 1024, 1024], P('dp', 'blk')
- grad_gain: float32 [2, 1024], replicated
- grad_shift: float32 [2, 1024], replicated
- grad_a: float32 [1024, 384], P('dp')
- grad_a_ff: float32 [4096, 128], P('dp')
- grad_b: float32 [128, 8192], P(None, 'dp')
- grad_b_ff: float32 [128, 1024], P(None, 'dp')
- new_mean_a: float32 [1024, 384], P('dp')
- new_square_a: float32 [1024, 384], P('dp')
- new_mean_a_ff: float32 [4096, 128], P('dp')
- new_square_a_ff: float32 [4096, 128], P('dp')
- new_mean_b: float32 [128, 8192], P(None, 'dp')
- new_square_b: float32 [128, 8192], P(None, 'dp')
- new_mean_b_ff: float32 [128, 1024], P(None, 'dp')
- new_square_b_ff: float32 [128, 1024], P(None, 'dp')
- folded_input_weights: bfloat16 [1024, 8192], P('dp')
- folded_down_weight: bfloat16 [4096, 1024], P('dp')
All inputs are finite; a program needn't handle non-finite values. No bound on the sum of `keep_a` or of `keep_a_ff` or of `keep_b` or of `keep_b_ff` on one device may be relied on, other than what follows from the above.
Results may differ from a plain program's by a relative error of at most 0.025.
Values may be sent and summed in bfloat16 or wider, within the bound.
A program may use at most 320 MiB of HBM per device.

v0:
```python
import math
import jax
import jax.numpy as jnp
from jax import lax
from jax.sharding import PartitionSpec as P

HEADS = 16
ROTARY = 16
DOMAINS = 22
highest = lax.Precision.HIGHEST
adapter_scale = 0.25
rope_base = 10000.0
norm_eps = 1e-05
masked_score = -1e30
first_fix = 1.0 - (0.9**10) ** 10
second_fix = 1.0 - (0.999**10) ** 10


def matrix_product(left, right):
    return jnp.dot(left, right, preferred_element_type=jnp.float32)


def product_right_transposed(left, right):
    return lax.dot_general(
        left, right, (((1,), (1,)), ((), ())), preferred_element_type=jnp.float32
    )


def product_left_transposed(left, right):
    return lax.dot_general(
        left, right, (((0,), (0,)), ((), ())), preferred_element_type=jnp.float32
    )


def precise_product(left, right):
    return jnp.dot(left, right, precision=highest)


def layer_norm(values, gain, shift):
    centre = values - jnp.mean(values, axis=-1, keepdims=True)
    spread = jnp.mean(centre * centre, axis=-1, keepdims=True)
    return centre * lax.rsqrt(spread + norm_eps) * gain + shift


def exact_gelu(values):
    return jax.nn.gelu(values, approximate=False)


def rope_tables(positions, rotary):
    half = rotary // 2
    freqs = rope_base ** (-(jnp.arange(half, dtype=jnp.float32) * 2.0) / rotary)
    angles = positions.astype(jnp.float32)[:, None] * freqs[None, :]
    return (jnp.cos(angles), jnp.sin(angles))


def rotate(values, cosine, sine, rotary):
    half = rotary // 2
    front = values[..., :half]
    back = values[..., half:rotary]
    rest = values[..., rotary:]
    cos_b = cosine[:, None, :]
    sin_b = sine[:, None, :]
    return jnp.concatenate(
        [front * cos_b - back * sin_b, back * cos_b + front * sin_b, rest], axis=-1
    )


def project(input_rows, weight_matrix, bias_vector, down, upper_factor):
    middle_rows = matrix_product(input_rows, down).astype(jnp.bfloat16)
    return (
        matrix_product(input_rows, weight_matrix)
        + bias_vector.astype(jnp.float32)
        + adapter_scale * matrix_product(middle_rows, upper_factor),
        middle_rows,
    )


def project_back(
    output_gradient, input_rows, middle_rows, weight_matrix, bias_vector, down, upper_factor
):
    middle_gradient = (
        adapter_scale * product_right_transposed(output_gradient, upper_factor)
    ).astype(jnp.bfloat16)
    upper_gradient = adapter_scale * product_left_transposed(middle_rows, output_gradient)
    grad_down = product_left_transposed(input_rows, middle_gradient)
    grad_in = product_right_transposed(output_gradient, weight_matrix) + product_right_transposed(
        middle_gradient, down
    )
    return (grad_in, grad_down, upper_gradient)


def split_blocks(full, bias_in, bias_ff, width, rank):
    w_all, w_ff, a_all, a_ff, b_all, b_ff = full
    part_qkv = (w_all[:, : 3 * width], bias_in[: 3 * width], a_all[:, :rank], b_all[:, : 3 * width])
    part_att = (
        w_all[:, 3 * width : 4 * width],
        bias_in[3 * width : 4 * width],
        a_all[:, rank : 2 * rank],
        b_all[:, 3 * width : 4 * width],
    )
    part_up = (
        w_all[:, 4 * width :],
        bias_in[4 * width :],
        a_all[:, 2 * rank :],
        b_all[:, 4 * width :],
    )
    part_ff = (w_ff, bias_ff, a_ff, b_ff)
    return (part_qkv, part_att, part_up, part_ff)


def adam_update(param, grad, mean, square, keep):
    mean_new = 0.9 * mean + 0.1 * grad
    square_new = 0.999 * square + 0.001 * grad * grad
    fresh = param - 0.01 * (mean_new / first_fix) / (jnp.sqrt(square_new / second_fix) + 1e-08)
    kept = keep.astype(jnp.float32)
    return (fresh, mean_new * kept, square_new * kept)


def body(
    tokens,
    cotangent,
    domain_ids,
    domain_weight,
    frozen_input_weights,
    bias_in,
    frozen_down_weight,
    bias_ff,
    norm_gain,
    norm_shift,
    adapt_a,
    adapt_a_ff,
    adapt_b,
    adapt_b_ff,
    mean_a,
    mean_a_ff,
    mean_b,
    mean_b_ff,
    square_a,
    square_a_ff,
    square_b,
    square_b_ff,
    keep_a,
    keep_a_ff,
    keep_b,
    keep_b_ff,
):
    seqs, span, width = tokens.shape
    rows = seqs * span
    rank = adapt_b.shape[0]
    depth = width // HEADS
    att_scale = 1.0 / math.sqrt(depth)
    shards = (
        frozen_input_weights,
        frozen_down_weight,
        adapt_a.astype(jnp.bfloat16),
        adapt_a_ff.astype(jnp.bfloat16),
        adapt_b.astype(jnp.bfloat16),
        adapt_b_ff.astype(jnp.bfloat16),
    )
    whole = (
        lax.all_gather(shards[0], "dp", axis=0, tiled=True),
        lax.all_gather(shards[1], "dp", axis=0, tiled=True),
        lax.all_gather(shards[2], "dp", axis=0, tiled=True),
        lax.all_gather(shards[3], "dp", axis=0, tiled=True),
        lax.all_gather(shards[4], "dp", axis=1, tiled=True),
        lax.all_gather(shards[5], "dp", axis=1, tiled=True),
    )
    part_qkv, part_att, part_up, part_ff = split_blocks(whole, bias_in, bias_ff, width, rank)
    input_rows = tokens.astype(jnp.float32).reshape(rows, width)
    first_f, first_pull = jax.vjp(layer_norm, input_rows, norm_gain[0], norm_shift[0])
    second_f, second_pull = jax.vjp(layer_norm, input_rows, norm_gain[1], norm_shift[1])
    first = first_f.astype(jnp.bfloat16)
    second = second_f.astype(jnp.bfloat16)
    joint, middle_qkv = project(first, *part_qkv)
    joint3 = joint.reshape(seqs, span, 3 * width)
    positions = lax.axis_index("blk") * span + jnp.arange(span, dtype=jnp.int32)
    cosine, sine = rope_tables(positions, ROTARY)

    def turn(query_raw, key_raw):
        return (rotate(query_raw, cosine, sine, ROTARY), rotate(key_raw, cosine, sine, ROTARY))

    (query_r, key_r), rope_pull = jax.vjp(
        turn,
        joint3[..., :width].reshape(seqs, span, HEADS, depth),
        joint3[..., width : 2 * width].reshape(seqs, span, HEADS, depth),
    )
    query_b = query_r.astype(jnp.bfloat16)
    key_local = key_r.astype(jnp.bfloat16)
    value_local = joint3[..., 2 * width :].reshape(seqs, span, HEADS, depth).astype(jnp.bfloat16)
    key_send = key_local.reshape(seqs, span, width)
    value_send = value_local.reshape(seqs, span, width)
    top = jnp.full((seqs, HEADS, span), masked_score, jnp.float32)
    key_piece = lax.all_gather(key_send, "blk", axis=1, tiled=True)
    value_piece = lax.all_gather(value_send, "blk", axis=1, tiled=True)
    count = key_piece.shape[1]
    key_h = key_piece.reshape(seqs, count, HEADS, depth)
    value_h = value_piece.reshape(seqs, count, HEADS, depth)
    scores = (
        jnp.einsum("sqhe,skhe->shqk", query_b, key_h, preferred_element_type=jnp.float32)
        * att_scale
    )
    allowed = positions[:, None] >= jnp.arange(count, dtype=jnp.int32)[None, :]
    scores = jnp.where(allowed, scores, masked_score)
    new_top = jnp.maximum(top, jnp.max(scores, axis=-1))
    weights = jnp.where(allowed, jnp.exp(scores - new_top[..., None]), 0.0)
    total = jnp.sum(weights, axis=-1)
    update = jnp.einsum(
        "shqk,skhe->sqhe", weights.astype(jnp.bfloat16), value_h, preferred_element_type=jnp.float32
    )
    accum = update
    top, total, accum = (new_top, total, accum)
    attended_f = (accum / jnp.transpose(total, (0, 2, 1))[..., None]).reshape(rows, width)
    log_total = top + jnp.log(total)
    attended = attended_f.astype(jnp.bfloat16)
    branch_att, middle_att = project(attended, *part_att)
    up_pre, middle_up = project(second, *part_up)
    hidden_f, gelu_pull = jax.vjp(exact_gelu, up_pre)
    hidden = hidden_f.astype(jnp.bfloat16)
    branch_ff, middle_ff = project(hidden, *part_ff)
    mixed = (input_rows + branch_att + branch_ff).astype(jnp.bfloat16).reshape(seqs, span, width)
    lookup = (domain_ids[..., None] == jnp.arange(DOMAINS, dtype=jnp.int32)).astype(jnp.float32)
    row_weight = jnp.sum(lookup * domain_weight, axis=-1).reshape(rows, 1)
    row_grad = cotangent.astype(jnp.float32).reshape(rows, width) * row_weight
    grad_low = row_grad.astype(jnp.bfloat16)
    grad_hidden, grad_a_ffp, grad_b_ffp = project_back(grad_low, hidden, middle_ff, *part_ff)
    upper_gradient = gelu_pull(grad_hidden)[0].astype(jnp.bfloat16)
    grad_second, grad_a_up, grad_b_up = project_back(upper_gradient, second, middle_up, *part_up)
    grad_att_f, grad_a_att, grad_b_att = project_back(grad_low, attended, middle_att, *part_att)
    grad_att = grad_att_f.astype(jnp.bfloat16)
    grad_heads = grad_att.reshape(seqs, span, HEADS, depth)
    delta = jnp.transpose(
        jnp.sum(
            grad_heads.astype(jnp.float32) * attended_f.reshape(seqs, span, HEADS, depth), axis=-1
        ),
        (0, 2, 1),
    )
    key_piece = lax.all_gather(key_send, "blk", axis=1, tiled=True)
    value_piece = lax.all_gather(value_send, "blk", axis=1, tiled=True)
    count = key_piece.shape[1]
    key_h = key_piece.reshape(seqs, count, HEADS, depth)
    value_h = value_piece.reshape(seqs, count, HEADS, depth)
    scores = (
        jnp.einsum("sqhe,skhe->shqk", query_b, key_h, preferred_element_type=jnp.float32)
        * att_scale
    )
    allowed = positions[:, None] >= jnp.arange(count, dtype=jnp.int32)[None, :]
    weights = jnp.where(allowed, jnp.exp(scores - log_total[..., None]), 0.0)
    grad_w = jnp.einsum("sqhe,skhe->shqk", grad_heads, value_h, preferred_element_type=jnp.float32)
    grad_s = (weights * (grad_w - delta[..., None])).astype(jnp.bfloat16)
    grad_query = (
        jnp.einsum("shqk,skhe->sqhe", grad_s, key_h, preferred_element_type=jnp.float32) * att_scale
    )
    stats_lse, stats_delta = (
        lax.all_gather(log_total.astype(jnp.bfloat16), "blk", axis=2, tiled=True).astype(
            log_total.dtype
        ),
        lax.all_gather(delta.astype(jnp.bfloat16), "blk", axis=2, tiled=True).astype(delta.dtype),
    )
    query_piece = lax.all_gather(query_b.reshape(seqs, span, width), "blk", axis=1, tiled=True)
    grad_piece = lax.all_gather(grad_att.reshape(seqs, span, width), "blk", axis=1, tiled=True)
    count = query_piece.shape[1]
    query_h = query_piece.reshape(seqs, count, HEADS, depth)
    grad_h = grad_piece.reshape(seqs, count, HEADS, depth)
    scores = (
        jnp.einsum("sqhe,skhe->shqk", query_h, key_local, preferred_element_type=jnp.float32)
        * att_scale
    )
    allowed = jnp.arange(count, dtype=jnp.int32)[:, None] >= positions[None, :]
    weights = jnp.where(allowed, jnp.exp(scores - stats_lse[..., None]), 0.0)
    grad_v = jnp.einsum(
        "shqk,sqhe->skhe", weights.astype(jnp.bfloat16), grad_h, preferred_element_type=jnp.float32
    )
    grad_w = jnp.einsum("sqhe,skhe->shqk", grad_h, value_local, preferred_element_type=jnp.float32)
    grad_s = (weights * (grad_w - stats_delta[..., None])).astype(jnp.bfloat16)
    grad_k = (
        jnp.einsum("shqk,sqhe->skhe", grad_s, query_h, preferred_element_type=jnp.float32)
        * att_scale
    )
    grad_query_raw, grad_key_raw = rope_pull((grad_query, grad_k))
    grad_joint = jnp.concatenate(
        [
            grad_query_raw.reshape(rows, width),
            grad_key_raw.reshape(rows, width),
            grad_v.reshape(rows, width),
        ],
        axis=1,
    ).astype(jnp.bfloat16)
    grad_first, grad_a_qkv, grad_b_qkv = project_back(grad_joint, first, middle_qkv, *part_qkv)
    back_one = first_pull(grad_first)
    back_two = second_pull(grad_second)
    grad_tokens = (
        (row_grad + back_one[0] + back_two[0]).astype(jnp.bfloat16).reshape(seqs, span, width)
    )
    gain_part = jnp.stack([back_one[1], back_two[1]])
    shift_part = jnp.stack([back_one[2], back_two[2]])
    grad_a_part = jnp.concatenate([grad_a_qkv, grad_a_att, grad_a_up], axis=1)
    grad_b_part = jnp.concatenate([grad_b_qkv, grad_b_att, grad_b_up], axis=1)
    summed = lax.psum(
        (grad_a_part, grad_a_ffp, grad_b_part, grad_b_ffp, gain_part, shift_part), ("dp", "blk")
    )
    owner = lax.axis_index("dp")
    grad_a = lax.dynamic_slice_in_dim(summed[0], owner * adapt_a.shape[0], adapt_a.shape[0], 0)
    grad_a_ff = lax.dynamic_slice_in_dim(
        summed[1], owner * adapt_a_ff.shape[0], adapt_a_ff.shape[0], 0
    )
    grad_b = lax.dynamic_slice_in_dim(summed[2], owner * adapt_b.shape[1], adapt_b.shape[1], 1)
    grad_b_ff = lax.dynamic_slice_in_dim(
        summed[3], owner * adapt_b_ff.shape[1], adapt_b_ff.shape[1], 1
    )
    grad_gain = summed[4]
    grad_shift = summed[5]
    fresh_a, new_mean_a, new_square_a = adam_update(adapt_a, grad_a, mean_a, square_a, keep_a)
    reset_down_adapter_left, new_mean_a_ff, new_square_a_ff = adam_update(
        adapt_a_ff, grad_a_ff, mean_a_ff, square_a_ff, keep_a_ff
    )
    fresh_b, new_mean_b, new_square_b = adam_update(adapt_b, grad_b, mean_b, square_b, keep_b)
    reset_down_adapter_right, new_mean_b_ff, new_square_b_ff = adam_update(
        adapt_b_ff, grad_b_ff, mean_b_ff, square_b_ff, keep_b_ff
    )
    fresh_b_all, reset_down_right_stacked = (
        lax.all_gather(fresh_b.astype(jnp.bfloat16), "dp", axis=1, tiled=True).astype(
            fresh_b.dtype
        ),
        lax.all_gather(
            reset_down_adapter_right.astype(jnp.bfloat16), "dp", axis=1, tiled=True
        ).astype(reset_down_adapter_right.dtype),
    )
    input_weight_update = jnp.concatenate(
        [
            precise_product(fresh_a[:, :rank], fresh_b_all[:, : 3 * width]),
            precise_product(fresh_a[:, rank : 2 * rank], fresh_b_all[:, 3 * width : 4 * width]),
            precise_product(fresh_a[:, 2 * rank :], fresh_b_all[:, 4 * width :]),
        ],
        axis=1,
    )
    folded_input_weights = (
        frozen_input_weights.astype(jnp.float32) + adapter_scale * input_weight_update
    ).astype(jnp.bfloat16)
    folded_down_weight = (
        frozen_down_weight.astype(jnp.float32)
        + adapter_scale * precise_product(reset_down_adapter_left, reset_down_right_stacked)
    ).astype(jnp.bfloat16)
    return (
        mixed,
        grad_tokens,
        grad_gain,
        grad_shift,
        grad_a,
        grad_a_ff,
        grad_b,
        grad_b_ff,
        new_mean_a,
        new_square_a,
        new_mean_a_ff,
        new_square_a_ff,
        new_mean_b,
        new_square_b,
        new_mean_b_ff,
        new_square_b_ff,
        folded_input_weights,
        folded_down_weight,
    )


def solution(mesh):
    in_specs = (
        P("dp", "blk", None),
        P("dp", "blk", None),
        P("dp", "blk"),
        P(),
        P("dp", None),
        P(),
        P("dp", None),
        P(),
        P(),
        P(),
        P("dp", None),
        P("dp", None),
        P(None, "dp"),
        P(None, "dp"),
        P("dp", None),
        P("dp", None),
        P(None, "dp"),
        P(None, "dp"),
        P("dp", None),
        P("dp", None),
        P(None, "dp"),
        P(None, "dp"),
        P("dp", None),
        P("dp", None),
        P(None, "dp"),
        P(None, "dp"),
    )
    out_specs = (
        P("dp", "blk", None),
        P("dp", "blk", None),
        P(),
        P(),
        P("dp", None),
        P("dp", None),
        P(None, "dp"),
        P(None, "dp"),
        P("dp", None),
        P("dp", None),
        P("dp", None),
        P("dp", None),
        P(None, "dp"),
        P(None, "dp"),
        P(None, "dp"),
        P(None, "dp"),
        P("dp", None),
        P("dp", None),
    )
    return jax.shard_map(body, mesh=mesh, in_specs=in_specs, out_specs=out_specs, check_vma=False)
```

profile of v0, /device:TPU:0, one launch (start us, length us, event | category | flops | bytes accessed | tf_op | source)
XLA Modules:
  0.0 990.2 jit_solution(3469510999970349865)
XLA Ops:
  12.5 12.9 %all_gather.45 = bf16[1024,384]{1,0:T(8,128)(2,1)} all-gather(bf16[128,384]{1,0:T(8,128)(2,1)S(1)} %convert_element_type.174), channel_id=1, replica_groups=mesh['dp'=8,'blk'=4] {'dp'}, dimensions={0}, use_global_device_ids=true | all-gather | bytes 884736 | tf_op jit(solution)/shard_map/all_gather | solution.py:163
  30.0 72.5 %all-gather.10.cloned.1.call-done = bf16[1024,8192]{1,0:T(8,128)(2,1)} async-done(((bf16[128,8192]{1,0:T(8,128)(2,1)}), bf16[1024,8192]{1,0:T(8,128)(2,1)}) %all-gather.10.cloned.1.call-update) | async-done | bytes 16777232 | tf_op jit(solution)/shard_map/all_gather | solution.py:161
  102.5 10.2 %fusion.23 = f32[768,3072]{1,0:T(8,128)} fusion(bf16[768,1024]{1,0:T(8,128)(2,1)S(1)} %get-tuple-element.112, bf16[1024,8192]{1,0:T(8,128)(2,1)} %all-gather.10.cloned.1.call-done), kind=kOutput, calls=%fused_computation.39 | convolution fusion | flops 4831838208 | bytes 17301504 | tf_op jit(solution)/shard_map/dot_general | solution.py:20
  112.8 20.2 %all-gather.12.cloned.1.call-done = bf16[128,8192]{1,0:T(8,128)(2,1)} async-done(((bf16[128,1024]{1,0:T(8,128)(2,1)}), bf16[128,8192]{1,0:T(8,128)(2,1)}) %all-gather.12.cloned.1.call-update) | async-done | bytes 2097168 | tf_op jit(solution)/shard_map/all_gather | solution.py:165
  132.9 5.3 multiply_add_fusion.1
  168.0 10.3 %all_gather.51 = bf16[128,1024]{1,0:T(8,128)(2,1)S(1)} all-gather(bf16[128,128]{1,0:T(8,128)(2,1)} %convert_element_type.194), channel_id=1, replica_groups=mesh['dp'=8,'blk'=4] {'dp'}, dimensions={1}, use_global_device_ids=true | all-gather | bytes 294912 | tf_op jit(solution)/shard_map/all_gather | solution.py:166
  190.3 12.6 %fusion.136 = f32[768,4096]{1,0:T(8,128)} fusion(bf16[768,1024]{1,0:T(8,128)(2,1)S(1)} %fusion.28, bf16[4096,1024]{1,0:T(8,128)(2,1)} %all-gather.18.cloned.1.call-done), kind=kOutput, calls=%fused_computation.232 | convolution fusion | flops 6442450944 | bytes 22544384 | tf_op jit(solution)/shard_map/dot_general | solution.py:24
  222.1 9.4 fusion.19
  231.5 31.8 %multiply_convert_fusion.2 = (bf16[768,4096]{1,0:T(8,128)(2,1)}, f32[768,4096]{1,0:T(8,128)}, f32[768,4096]{1,0:T(8,128)}) fusion(bf16[768,128]{1,0:T(8,128)(2,1)S(1)} %copy-done.54, bf16[128,8192]{1,0:T(8,128)(2,1)S(1)} %copy-done.56, f32[768,4096]{1,0:T(8,128)S(1)} %fusion.19, f32[4096]{0:T(1024)S(1)} %copy-done.84), kind=kOutput, calls=%fused_computation.15 | convolution fusion | flops 1019215872 | bytes 45301760 | tf_op jit(solution)/shard_map/dot_general | solution.py:20
  263.4 17.3 %add_convert_fusion = bf16[768,4096]{1,0:T(8,128)(2,1)} fusion(f32[768,4096]{1,0:T(8,128)} %get-tuple-element.99, f32[768,4096]{1,0:T(8,128)} %fusion.136, f32[768,4096]{1,0:T(8,128)} %get-tuple-element.136, bf16[768,128]{1,0:T(8,128)(2,1)} %fusion.69, bf16[4096,128]{1,0:T(8,128)(2,1)} %all-gather.20.cloned.1.call-done), kind=kOutput, calls=%fused_computation.14 | convolution fusion | flops 852492288 | bytes 45285376 | tf_op jit(solution)/shard_map/dot_general | solution.py:24
  298.8 12.6 %fusion.135 = f32[768,1024]{1,0:T(8,128)} fusion(bf16[768,4096]{1,0:T(8,128)(2,1)} %get-tuple-element.98, bf16[4096,1024]{1,0:T(8,128)(2,1)} %all-gather.18.cloned.1.call-done), kind=kOutput, calls=%fused_computation.231 | convolution fusion | flops 6442450944 | bytes 17825792 | tf_op jit(solution)/shard_map/dot_general | solution.py:20
  311.4 21.1 %all-gather.16.cloned.1.call-done = bf16[3,1024,1024]{1,2,0:T(8,128)(2,1)} async-done(((bf16[3,256,1024]{1,2,0:T(8,128)(2,1)}), bf16[3,1024,1024]{1,2,0:T(8,128)(2,1)}) %all-gather.16.cloned.1.call-update) | async-done | bytes 6291472 | tf_op jit(solution)/shard_map/all_gather | solution.py:193
  332.5 21.8 %select_reduce_fusion = (f32[3,16,256]{2,1,0:T(8,128)S(1)}, f32[3,16,256,1024]{3,2,1,0:T(8,128)}) fusion(pred[256,1024]{1,0:T(8,128)(4,1)S(1)} %copy-done.5, bf16[3,1024,16,64]{1,3,2,0:T(8,128)(2,1)} %bitcast.174, bf16[3,256,16,48]{1,3,2,0:T(8,128)(2,1)S(1)} %copy-done.14, bf16[3,256,16,8]{1,3,2,0:T(8,128)(2,1)S(1)} %get-tuple-element.124, ...), kind=kOutput, calls=%fused_computation.4 | convolution fusion | flops 1653067776 | bytes 58507264 | tf_op jit(solution)/shard_map/sqhe,skhe->shqk/dot_general | solution.py:199
  354.3 23.0 %fusion.1 = f32[3,16,256]{2,1,0:T(8,128)S(1)} fusion(f32[3,16,256,1024]{3,2,1,0:T(8,128)} %get-tuple-element.135, f32[3,16,256]{2,1,0:T(8,128)S(1)} %broadcast_maximum_fusion, pred[256,1024]{1,0:T(8,128)(4,1)S(1)} %copy-done.5), kind=kLoop, calls=%fused_computation.6 | loop fusion | flops 62902272 | bytes 50692096 | tf_op jit(solution)/shard_map/reduce_sum | solution.py:206
  377.3 20.7 %all_gather.53 = bf16[3,16,1024]{2,1,0:T(8,128)(2,1)S(1)} all-gather(bf16[3,16,256]{2,1,0:T(8,128)(2,1)S(1)} %get-tuple-element.96), channel_id=1, replica_groups=mesh['dp'=8,'blk'=4] {'blk'}, dimensions={2}, use_global_device_ids=true | all-gather | bytes 122880 | tf_op jit(solution)/shard_map/all_gather | solution.py:254
  398.0 50.5 %all-gather.14.cloned.1.call-done = bf16[3,1024,1024]{1,2,0:T(8,128)(2,1)} async-done(((bf16[3,256,1024]{1,2,0:T(8,128)(2,1)}), bf16[3,1024,1024]{1,2,0:T(8,128)(2,1)}) %all-gather.14.cloned.1.call-update) | async-done | bytes 6291472 | tf_op jit(solution)/shard_map/all_gather | solution.py:194
  448.5 23.5 %multiply_reduce_fusion = (f32[3,256,16]{1,2,0:T(8,128)S(1)}, bf16[3,256,16,64]{1,3,2,0:T(8,128)(2,1)}) fusion(bf16[3,256,16,64]{1,3,2,0:T(8,128)(2,1)S(1)} %copy-done.39, f32[3,256,16]{1,2,0:T(8,128)S(1)} %bitcast.202, bf16[3,1024,16,64]{1,3,2,0:T(8,128)(2,1)} %bitcast.218, f32[3,16,256,1024]{3,2,1,0:T(8,128)} %get-tuple-element.135, ...), kind=kOutput, calls=%fused_computation.86 | convolution fusion | flops 1677447168 | bytes 60178432 | tf_op jit(solution)/shard_map/shqk,skhe->sqhe/dot_general | solution.py:207
  472.1 28.8 %multiply_bitcast_fusion.1 = f32[3,256,16,64]{1,3,2,0:T(8,128)} fusion(bf16[3,1024,16,64]{1,3,2,0:T(8,128)(2,1)} %bitcast.175, f32[3,16,256,1024]{3,2,1,0:T(8,128)} %get-tuple-element.135, bf16[3,256,16,64]{1,3,2,0:T(8,128)(2,1)S(1)} %copy-done.39, bf16[3,1024,16,64]{1,3,2,0:T(8,128)(2,1)} %bitcast.219, f32[3,16,256]{2,1,0:T(8,128)S(1)} %bitcast.211, ...), kind=kOutput, calls=%fused_computation.85 | convolution fusion | flops 3297509376 | bytes 67993600 | tf_op jit(solution)/shard_map/shqk,skhe->sqhe/dot_general | solution.py:251
  500.9 27.6 %all_gather.55 = bf16[3,16,1024]{2,1,0:T(8,128)(2,1)S(1)} all-gather(bf16[3,16,256]{2,1,0:T(8,128)(2,1)S(1)} %bitcast_convert_fusion), channel_id=1, replica_groups=mesh['dp'=8,'blk'=4] {'blk'}, dimensions={2}, use_global_device_ids=true | all-gather | bytes 122880 | tf_op jit(solution)/shard_map/all_gather | solution.py:257
  529.2 35.5 %all-gather.22.cloned.1.call-done = bf16[3,1024,1024]{1,2,0:T(8,128)(2,1)} async-done(((bf16[3,256,1024]{1,2,0:T(8,128)(2,1)}), bf16[3,1024,1024]{1,2,0:T(8,128)(2,1)}) %all-gather.22.cloned.1.call-update) | async-done | bytes 6291472 | tf_op jit(solution)/shard_map/all_gather | solution.py:259
  564.7 22.0 %fusion.134 = f32[3,16,1024,256]{3,2,1,0:T(8,128)} fusion(bf16[3,1024,16,64]{1,3,2,0:T(8,128)(2,1)} %bitcast.179, bf16[3,256,16,48]{1,3,2,0:T(8,128)(2,1)S(1)} %copy-done.13, bf16[3,256,16,8]{1,3,2,0:T(8,128)(2,1)S(1)} %copy-done.36, bf16[3,256,16,8]{1,3,2,0:T(8,128)(2,1)S(1)} %copy-done.34), kind=kOutput, calls=%fused_computation.230 | convolution fusion | flops 1615331328 | bytes 58195968 | tf_op jit(solution)/shard_map/sqhe,skhe->shqk/dot_general | solution.py:265
  586.7 93.3 %all-gather.24.cloned.1.call-done = bf16[3,1024,1024]{2,1,0:T(8,128)(2,1)} async-done(((bf16[3,256,1024]{2,1,0:T(8,128)(2,1)}), bf16[3,1024,1024]{2,1,0:T(8,128)(2,1)}) %all-gather.24.cloned.1.call-update) | async-done | bytes 6291472 | tf_op jit(solution)/shard_map/all_gather | solution.py:260
  680.1 8.7 copy.80
  688.7 20.5 %fusion.64 = bf16[3,256,16,64]{1,3,2,0:T(8,128)(2,1)} fusion(bf16[3,1024,16,64]{1,3,2,0:T(8,128)(2,1)} %bitcast.189, f32[3,16,1024,256]{3,2,1,0:T(8,128)} %fusion.134, f32[3,16,1024]{2,1,0:T(8,128)S(1)} %convert_element_type.203, pred[1024,256]{1,0:T(8,128)(4,1)S(1)} %copy-done.60), kind=kOutput, calls=%fused_computation.97 | convolution fusion | flops 1661730816 | bytes 58654720 | tf_op jit(solution)/shard_map/shqk,sqhe->skhe/dot_general | solution.py:270
  709.2 28.0 %multiply_bitcast_fusion = f32[3,256,16,64]{1,3,2,0:T(8,128)} fusion(bf16[3,1024,16,64]{1,3,2,0:T(8,128)(2,1)} %bitcast.180, f32[3,16,1024,256]{3,2,1,0:T(8,128)} %fusion.134, bf16[3,1024,16,64]{1,3,2,0:T(8,128)(2,1)} %bitcast.190, bf16[3,256,16,64]{1,3,2,0:T(8,128)(2,1)} %bitcast.191, f32[3,16,1024]{2,1,0:T(8,128)} %convert_element_type.206, ...), kind=kOutput, calls=%fused_computation.83 | convolution fusion | flops 3297509376 | bytes 68288512 | tf_op jit(solution)/shard_map/shqk,sqhe->skhe/dot_general | solution.py:276
  761.6 8.6 fusion.21
  772.9 13.2 %fusion.128 = (f32[1024]{0:T(1024)S(1)}, f32[768]{0:T(1024)S(1)}, f32[768]{0:T(1024)S(1)}, f32[1024]{0:T(1024)S(1)}, f32[768,1024]{1,0:T(8,128)S(1)}) fusion(f32[1024]{0:T(1024)S(1)} %bitcast.208, f32[768]{0:T(1024)S(1)} %copy-done.71, bf16[3,256,1024]{2,1,0:T(8,128)(2,1)S(1)} %copy-done.1, f32[768,1024]{1,0:T(8,128)S(1)} %convolution_add_fusion, ...), kind=kOutput, calls=%fused_computation.225 | convolution fusion | flops 6451097600 | bytes 25715712 | tf_op jit(solution)/shard_map/dot_general | solution.py:24
  789.1 39.3 %all-reduce.6 = (f32[2,1024]{1,0:T(2,128)}, f32[2,1024]{1,0:T(2,128)}) all-reduce(f32[2,1024]{1,0:T(2,128)S(1)} %pad_maximum_fusion.2, f32[2,1024]{1,0:T(2,128)S(1)} %pad_maximum_fusion.3), channel_id=1, replica_groups=mesh['dp'=8,'blk'=4] {'dp','blk'}, use_global_device_ids=true, to_apply=%region_12.13 | all-reduce | flops 4096 | bytes 32768 | tf_op jit(solution)/shard_map/psum | solution.py:298
  831.5 5.1 fusion.59
  836.6 103.6 %all-reduce.10.cloned.1.call-done = (f32[1024,384]{0,1:T(8,128)}, f32[4096,128]{1,0:T(8,128)}, f32[128,8192]{1,0:T(8,128)}, f32[128,1024]{1,0:T(8,128)}) async-done(((f32[1024,384]{0,1:T(8,128)}, f32[4096,128]{1,0:T(8,128)}, f32[128,8192]{1,0:T(8,128)}, f32[128,1024]{1,0:T(8,128)}), (f32[1024,384]{0,1:T(8,128)}, f32[4096,128]{1,0:T(8,128)}, f32[128,8192]{1,0:T(8,128)}, ...) | async-done | bytes 8388624 | tf_op jit(solution)/shard_map/psum | solution.py:298
  942.9 6.1 fusion.51
  957.2 10.1 %all_gather.57 = bf16[128,1024]{1,0:T(8,128)(2,1)S(1)} all-gather(bf16[128,128]{1,0:T(8,128)(2,1)S(1)} %get-tuple-element.88), channel_id=1, replica_groups=mesh['dp'=8,'blk'=4] {'dp'}, dimensions={1}, use_global_device_ids=true | all-gather | bytes 294912 | tf_op jit(solution)/shard_map/all_gather | solution.py:324
  (321 shorter events, 148.3 us)
Async XLA Ops:
  7.2 95.3 %all-gather.10.cloned.1.call-start = ((), (), s32[]{:S(2)}) async-start(), calls=%async_computation | async-start | bytes 18874368 | tf_op jit(solution)/shard_map/all_gather | solution.py:161
  8.0 125.0 %all-gather.12.cloned.1.call-start = ((), (), s32[]{:S(2)}) async-start(), calls=%async_computation.1 | async-start | bytes 2359296 | tf_op jit(solution)/shard_map/all_gather | solution.py:165
  9.9 180.5 %all-gather.18.cloned.1.call-start = ((), (), s32[]{:S(2)}) async-start(), calls=%async_computation.4 | async-start | bytes 9437184 | tf_op jit(solution)/shard_map/all_gather | solution.py:162
  10.6 252.8 %all-gather.20.cloned.1.call-start = ((), (), s32[]{:S(2)}) async-start(), calls=%async_computation.5 | async-start | bytes 1179648 | tf_op jit(solution)/shard_map/all_gather | solution.py:164
  11.4 321.1 %all-gather.16.cloned.1.call-start = ((), (), s32[]{:S(2)}) async-start(), calls=%async_computation.3 | async-start | bytes 7864320 | tf_op jit(solution)/shard_map/all_gather | solution.py:193
  28.1 84.6 %copy-start.21 = (bf16[768,1024]{1,0:T(8,128)(2,1)}, bf16[768,1024]{1,0:T(8,128)(2,1)S(1)}, u32[]{:S(2)}) copy-start(bf16[768,1024]{1,0:T(8,128)(2,1)S(1)} %get-tuple-element.112) | copy-start | bytes 4718596
  29.9 103.1 %copy-start.45 = (bf16[768,128]{1,0:T(8,128)(2,1)}, bf16[768,128]{1,0:T(8,128)(2,1)S(1)}, u32[]{:S(2)}) copy-start(bf16[768,128]{1,0:T(8,128)(2,1)S(1)} %convolution_convert_fusion.3) | copy-start | bytes 589828
  30.0 121.2 %copy-start.66 = (f32[256,8]{0,1:T(8,128)}, f32[256,8]{0,1:T(8,128)S(1)}, u32[]{:S(2)}) copy-start(f32[256,8]{0,1:T(8,128)S(1)} %get-tuple-element.132) | copy-start | bytes 24580
  30.0 121.2 %copy-start.68 = (f32[256,8]{0,1:T(8,128)}, f32[256,8]{0,1:T(8,128)S(1)}, u32[]{:S(2)}) copy-start(f32[256,8]{0,1:T(8,128)S(1)} %get-tuple-element.133) | copy-start | bytes 24580
  154.7 293.8 %all-gather.14.cloned.1.call-start = ((), (), s32[]{:S(2)}) async-start(), calls=%async_computation.2 | async-start | bytes 7864320 | tf_op jit(solution)/shard_map/all_gather | solution.py:194
  158.5 26.3 %copy-start.19 = (bf16[3,256,1024]{2,1,0:T(8,128)(2,1)S(1)}, bf16[3,256,1024]{2,1,0:T(8,128)(2,1)}, u32[]{:S(2)}) copy-start(bf16[3,256,1024]{2,1,0:T(8,128)(2,1)} %param.27) | copy-start | bytes 4718596
  158.6 406.2 %all-gather.22.cloned.1.call-start = ((), (), s32[]{:S(2)}) async-start(), calls=%async_computation.6 | async-start | bytes 7864320 | tf_op jit(solution)/shard_map/all_gather | solution.py:259
  185.2 103.5 %copy-start.6 = (bf16[768,1024]{1,0:T(8,128)(2,1)}, bf16[768,1024]{1,0:T(8,128)(2,1)S(1)}, u32[]{:S(2)}) copy-start(bf16[768,1024]{1,0:T(8,128)(2,1)S(1)} %fusion.28) | copy-start | bytes 4718596
  221.8 458.3 %all-gather.24.cloned.1.call-start = ((), (), s32[]{:S(2)}) async-start(), calls=%async_computation.7 | async-start | bytes 7864320 | tf_op jit(solution)/shard_map/all_gather | solution.py:260
  298.7 33.7 %copy-start.5 = (pred[256,1024]{1,0:T(8,128)(4,1)S(1)}, pred[256,1024]{1,0:T(8,128)(4,1)}, u32[]{:S(2)}) copy-start(pred[256,1024]{1,0:T(8,128)(4,1)} %iota_compare_fusion.1) | copy-start | bytes 786436
  298.7 33.7 %copy-start.14 = (bf16[3,256,16,48]{1,3,2,0:T(8,128)(2,1)S(1)}, bf16[3,256,16,48]{1,3,2,0:T(8,128)(2,1)}, u32[]{:S(2)}) copy-start(bf16[3,256,16,48]{1,3,2,0:T(8,128)(2,1)} %slice.131) | copy-start | bytes 3538948
  298.7 641.4 %all-reduce.10.cloned.1.call-start = ((), (), s32[]{:S(2)}) async-start(), calls=%async_computation.9 | async-start | bytes 16777216 | tf_op jit(solution)/shard_map/psum | solution.py:298
  354.3 94.2 %copy-start.39 = (bf16[3,256,16,64]{1,3,2,0:T(8,128)(2,1)S(1)}, bf16[3,256,16,64]{1,3,2,0:T(8,128)(2,1)}, u32[]{:S(2)}) copy-start(bf16[3,256,16,64]{1,3,2,0:T(8,128)(2,1)} %copy.77) | copy-start | bytes 4718596
  398.0 290.7 %copy-start.64 = (f32[3,16,1024]{2,1,0:T(8,128)}, f32[3,16,1024]{2,1,0:T(8,128)S(1)}, u32[]{:S(2)}) copy-start(f32[3,16,1024]{2,1,0:T(8,128)S(1)} %convert_element_type.203) | copy-start | bytes 589828
  500.9 63.8 %copy-start.13 = (bf16[3,256,16,48]{1,3,2,0:T(8,128)(2,1)S(1)}, bf16[3,256,16,48]{1,3,2,0:T(8,128)(2,1)}, u32[]{:S(2)}) copy-start(bf16[3,256,16,48]{1,3,2,0:T(8,128)(2,1)} %copy-done.12) | copy-start | bytes 3538948
  500.9 63.8 %copy-start.34 = (bf16[3,256,16,8]{1,3,2,0:T(8,128)(2,1)S(1)}, bf16[3,256,16,8]{1,3,2,0:T(8,128)(2,1)}, u32[]{:S(2)}) copy-start(bf16[3,256,16,8]{1,3,2,0:T(8,128)(2,1)} %copy-done.33) | copy-start | bytes 589828
  500.9 63.8 %copy-start.36 = (bf16[3,256,16,8]{1,3,2,0:T(8,128)(2,1)S(1)}, bf16[3,256,16,8]{1,3,2,0:T(8,128)(2,1)}, u32[]{:S(2)}) copy-start(bf16[3,256,16,8]{1,3,2,0:T(8,128)(2,1)} %copy-done.35) | copy-start | bytes 589828
  586.7 102.0 %copy-start.60 = (pred[1024,256]{1,0:T(8,128)(4,1)S(1)}, pred[1024,256]{1,0:T(8,128)(4,1)}, u32[]{:S(2)}) copy-start(pred[1024,256]{1,0:T(8,128)(4,1)} %iota_compare_fusion) | copy-start | bytes 786436
  709.2 28.0 %copy-start.15 = (f32[3,256,16,64]{1,3,2,0:T(8,128)S(1)}, f32[3,256,16,64]{1,3,2,0:T(8,128)}, u32[]{:S(2)}) copy-start(f32[3,256,16,64]{1,3,2,0:T(8,128)} %multiply_bitcast_fusion.1) | copy-start | bytes 9437188
  709.2 28.0 %copy-start.67 = (f32[256,8]{0,1:T(8,128)S(1)}, f32[256,8]{0,1:T(8,128)}, u32[]{:S(2)}) copy-start(f32[256,8]{0,1:T(8,128)} %copy-done.66) | copy-start | bytes 24580
  709.2 28.0 %copy-start.69 = (f32[256,8]{0,1:T(8,128)S(1)}, f32[256,8]{0,1:T(8,128)}, u32[]{:S(2)}) copy-start(f32[256,8]{0,1:T(8,128)} %copy-done.68) | copy-start | bytes 24580
  761.6 215.2 %all-gather.26.cloned.1.call-start = ((), (), s32[]{:S(2)}) async-start(), calls=%async_computation.8 | async-start | bytes 2359296 | tf_op jit(solution)/shard_map/all_gather | solution.py:321
  836.6 106.2 %copy-start.41 = (bf16[128,1024]{1,0:T(8,128)(2,1)S(1)}, bf16[128,1024]{1,0:T(8,128)(2,1)}, u32[]{:S(2)}) copy-start(bf16[128,1024]{1,0:T(8,128)(2,1)} %copy-done.40) | copy-start | bytes 786436
  836.6 106.2 %copy-start.53 = (bf16[768,128]{1,0:T(8,128)(2,1)S(1)}, bf16[768,128]{1,0:T(8,128)(2,1)}, u32[]{:S(2)}) copy-start(bf16[768,128]{1,0:T(8,128)(2,1)} %copy-done.52) | copy-start | bytes 589828
  836.6 106.2 %copy-start.82 = (f32[1024]{0:T(1024)S(1)}, f32[1024]{0:T(1024)}, u32[]{:S(2)}) copy-start(f32[1024]{0:T(1024)} %convert_element_type.191) | copy-start | bytes 12292
  836.6 106.2 %copy-start.83 = (f32[1024]{0:T(1024)S(1)}, f32[1024]{0:T(1024)}, u32[]{:S(2)}) copy-start(f32[1024]{0:T(1024)} %slice_convert_fusion.2) | copy-start | bytes 12292
  942.8 29.6 %copy-start.30 = (f32[128,1024]{1,0:T(8,128)}, f32[128,1024]{1,0:T(8,128)S(1)}, u32[]{:S(2)}) copy-start(f32[128,1024]{1,0:T(8,128)S(1)} %get-tuple-element.93) | copy-start | bytes 1572868
  (73 other events, 552.0 us)
Sparse Core Ops, SparseCore 0:
  9.9 92.5 all-gather.9
  105.0 27.8 all-gather.11
  134.8 55.4 all-gather.17
  192.6 23.4 all-gather.19
  217.6 114.8 all-gather.15
  333.9 114.6 all-gather.13
  450.1 114.6 all-gather.21
  566.3 113.7 all-gather.23
  761.7 178.4 all-reduce.9
  942.9 28.6 all-gather.25
where the time goes:
time: 999 us; the launch traced here: 990 us
  waiting for transfers between devices  400 us (40%)
  matrix products  326 us (33%)
  blocking collectives  121 us (12%)
  other arithmetic  68.4 us (7%)
  local copies, waits for them, and re-layouts  58.5 us (6%)
  between operations  15.7 us (2%)
    psum x1, waiting for transfers between devices, body(): lax.psum((grad_a_part, grad_a_ffp, grad_b_part, grad_b_ffp, gain_part, sh...  104 us
    all_gather x1, waiting for transfers between devices, body(): lax.all_gather(grad_att.reshape(seqs, span, width), 'blk', axis=1, tiled=...  93.3 us
    dot_general x12, matrix products, matrix_product(): return jnp.dot(left, right, preferred_element_type=jnp.float32)  91.1 us
    dot_general x12, matrix products, product_right_transposed(): lax.dot_general(left, right, (((1,), (1,)), ((), ())), preferred_element_...  72.7 us
    all_gather x1, waiting for transfers between devices, body(): lax.all_gather(shards[0], 'dp', axis=0, tiled=True)  72.5 us
    all_gather x1, waiting for transfers between devices, body(): value_piece = lax.all_gather(value_send, 'blk', axis=1, tiled=True)  50.5 us
    psum x1, blocking collectives, body(): lax.psum((grad_a_part, grad_a_ffp, grad_b_part, grad_b_ffp, gain_part, sh...  39.3 us
    all_gather x1, waiting for transfers between devices, body(): lax.all_gather(query_b.reshape(seqs, span, width), 'blk', axis=1, tiled=T...  35.5 us
  transfers between devices with their start and end apart: 10, of which 8 were waited for; matrix products, arithmetic and copies ran while one was open for 36% of the time, Pallas kernels for 0%

commit v1 on v0

--- a/solution.py
+++ b/solution.py
@@ -296,7 +296,8 @@
     grad_a_part = jnp.concatenate([grad_a_qkv, grad_a_att, grad_a_up], axis=1)
     grad_b_part = jnp.concatenate([grad_b_qkv, grad_b_att, grad_b_up], axis=1)
     summed = lax.psum(
-        (grad_a_part, grad_a_ffp, grad_b_part, grad_b_ffp, gain_part, shift_part), ("dp", "blk")
+        lax.psum((grad_a_part, grad_a_ffp, grad_b_part, grad_b_ffp, gain_part, shift_part), "blk"),
+        "dp",
     )
     owner = lax.axis_index("dp")
     grad_a = lax.dynamic_slice_in_dim(summed[0], owner * adapt_a.shape[0], adapt_a.shape[0], 0)

time: 999 us -> 1240 us (1.24)
  waiting for transfers between devices: 400 us -> 641 us
    psum x1, waiting for transfers between devices: 104 us -> 263 us  [body(): lax.psum((grad_a_part, grad_a_ffp, grad_b_part, grad_b_ffp, gain_part, sh...]
    psum x0 -> x1, waiting for transfers between devices: none -> 57.5 us  [body(): lax.psum(lax.psum((grad_a_part, grad_a_ffp, grad_b_part, grad_b_ffp, gain...]
    psum x0 -> x1, blocking collectives: none -> 24.1 us  [body(): lax.psum(lax.psum((grad_a_part, grad_a_ffp, grad_b_part, grad_b_ffp, gain...]
    psum x1, blocking collectives: 39.3 us -> 17.3 us  [body(): lax.psum((grad_a_part, grad_a_ffp, grad_b_part, grad_b_ffp, gain_part, sh...]
    all_gather x1, waiting for transfers between devices: 21.1 us -> 36.8 us  [body(): key_piece = lax.all_gather(key_send, 'blk', axis=1, tiled=True)]
  transfers between devices with their start and end apart: 10 -> 11, of which waited for: 8 -> 9; matrix products, arithmetic and copies ran while one was open for 36% -> 29% of each run, Pallas kernels for 0% -> 0%
where the time goes in v1:
time: 1240 us; the launch traced here: 1230 us
  waiting for transfers between devices  641 us (52%)
  matrix products  326 us (26%)
  blocking collectives  122 us (10%)
  other arithmetic  70.8 us (6%)
  local copies, waits for them, and re-layouts  54.5 us (4%)
  between operations  15.5 us (1%)
    psum x1, waiting for transfers between devices, body(): lax.psum((grad_a_part, grad_a_ffp, grad_b_part, grad_b_ffp, gain_part, sh...  263 us
    all_gather x1, waiting for transfers between devices, body(): lax.all_gather(grad_att.reshape(seqs, span, width), 'blk', axis=1, tiled=...  93.4 us
    dot_general x12, matrix products, matrix_product(): return jnp.dot(left, right, preferred_element_type=jnp.float32)  90.4 us
    dot_general x12, matrix products, product_right_transposed(): lax.dot_general(left, right, (((1,), (1,)), ((), ())), preferred_element_...  72.8 us
    all_gather x1, waiting for transfers between devices, body(): lax.all_gather(shards[0], 'dp', axis=0, tiled=True)  72.5 us
    psum x1, waiting for transfers between devices, body(): lax.psum(lax.psum((grad_a_part, grad_a_ffp, grad_b_part, grad_b_ffp, gain...  57.5 us
    all_gather x1, waiting for transfers between devices, body(): value_piece = lax.all_gather(value_send, 'blk', axis=1, tiled=True)  50.5 us
    all_gather x1, waiting for transfers between devices, body(): key_piece = lax.all_gather(key_send, 'blk', axis=1, tiled=True)  36.8 us
  transfers between devices with their start and end apart: 11, of which 9 were waited for; matrix products, arithmetic and copies ran while one was open for 29% of the time, Pallas kernels for 0%

profile of v1, /device:TPU:0, one launch (start us, length us, event | category | flops | bytes accessed | tf_op | source)
XLA Modules:
  0.0 1231.3 jit_solution(4336502659930537610)
XLA Ops:
  12.5 12.9 %all_gather.45 = bf16[1024,384]{1,0:T(8,128)(2,1)} all-gather(bf16[128,384]{1,0:T(8,128)(2,1)S(1)} %convert_element_type.174), channel_id=1, replica_groups=mesh['dp'=8,'blk'=4] {'dp'}, dimensions={0}, use_global_device_ids=true | all-gather | bytes 884736 | tf_op jit(solution)/shard_map/all_gather | solution.py:163
  30.0 72.5 %all-gather.10.cloned.1.call-done = bf16[1024,8192]{1,0:T(8,128)(2,1)} async-done(((bf16[128,8192]{1,0:T(8,128)(2,1)}), bf16[1024,8192]{1,0:T(8,128)(2,1)}) %all-gather.10.cloned.1.call-update) | async-done | bytes 16777232 | tf_op jit(solution)/shard_map/all_gather | solution.py:161
  102.5 10.2 fusion.23
  112.8 20.2 %all-gather.12.cloned.1.call-done = bf16[128,8192]{1,0:T(8,128)(2,1)} async-done(((bf16[128,1024]{1,0:T(8,128)(2,1)}), bf16[128,8192]{1,0:T(8,128)(2,1)}) %all-gather.12.cloned.1.call-update) | async-done | bytes 2097168 | tf_op jit(solution)/shard_map/all_gather | solution.py:165
  159.5 10.1 all_gather.51
  179.2 10.8 all-gather.18.cloned.1.call-done
  190.0 12.6 %fusion.136 = f32[768,4096]{1,0:T(8,128)} fusion(bf16[768,1024]{1,0:T(8,128)(2,1)S(1)} %fusion.28, bf16[4096,1024]{1,0:T(8,128)(2,1)} %all-gather.18.cloned.1.call-done), kind=kOutput, calls=%fused_computation.232 | convolution fusion | flops 6442450944 | bytes 22544384 | tf_op jit(solution)/shard_map/dot_general | solution.py:24
  221.8 9.4 fusion.19
  231.2 31.9 %multiply_convert_fusion.2 = (bf16[768,4096]{1,0:T(8,128)(2,1)}, f32[768,4096]{1,0:T(8,128)}, f32[768,4096]{1,0:T(8,128)}) fusion(bf16[768,128]{1,0:T(8,128)(2,1)S(1)} %copy-done.57, bf16[128,8192]{1,0:T(8,128)(2,1)S(1)} %copy-done.59, f32[768,4096]{1,0:T(8,128)S(1)} %fusion.19, f32[4096]{0:T(1024)S(1)} %copy-done.95), kind=kOutput, calls=%fused_computation.15 | convolution fusion | flops 1019215872 | bytes 45301760 | tf_op jit(solution)/shard_map/dot_general | solution.py:20
  263.1 17.2 %add_convert_fusion = bf16[768,4096]{1,0:T(8,128)(2,1)} fusion(f32[768,4096]{1,0:T(8,128)} %get-tuple-element.105, f32[768,4096]{1,0:T(8,128)} %fusion.136, f32[768,4096]{1,0:T(8,128)} %get-tuple-element.142, bf16[768,128]{1,0:T(8,128)(2,1)} %fusion.69, bf16[4096,128]{1,0:T(8,128)(2,1)} %all-gather.20.cloned.1.call-done), kind=kOutput, calls=%fused_computation.14 | convolution fusion | flops 852492288 | bytes 45285376 | tf_op jit(solution)/shard_map/dot_general | solution.py:24
  295.3 36.8 %all-gather.16.cloned.1.call-done = bf16[3,1024,1024]{1,2,0:T(8,128)(2,1)} async-done(((bf16[3,256,1024]{1,2,0:T(8,128)(2,1)}), bf16[3,1024,1024]{1,2,0:T(8,128)(2,1)}) %all-gather.16.cloned.1.call-update) | async-done | bytes 6291472 | tf_op jit(solution)/shard_map/all_gather | solution.py:193
  332.1 21.8 %select_reduce_fusion = (f32[3,16,256]{2,1,0:T(8,128)S(1)}, f32[3,16,256,1024]{3,2,1,0:T(8,128)}) fusion(pred[256,1024]{1,0:T(8,128)(4,1)S(1)} %copy-done.5, bf16[3,1024,16,64]{1,3,2,0:T(8,128)(2,1)} %bitcast.174, bf16[3,256,16,48]{1,3,2,0:T(8,128)(2,1)S(1)} %copy-done.14, bf16[3,256,16,8]{1,3,2,0:T(8,128)(2,1)S(1)} %get-tuple-element.130, ...), kind=kOutput, calls=%fused_computation.4 | convolution fusion | flops 1653067776 | bytes 58507264 | tf_op jit(solution)/shard_map/sqhe,skhe->shqk/dot_general | solution.py:199
  354.0 23.0 %fusion.1 = f32[3,16,256]{2,1,0:T(8,128)S(1)} fusion(f32[3,16,256,1024]{3,2,1,0:T(8,128)} %get-tuple-element.141, f32[3,16,256]{2,1,0:T(8,128)S(1)} %broadcast_maximum_fusion, pred[256,1024]{1,0:T(8,128)(4,1)S(1)} %copy-done.5), kind=kLoop, calls=%fused_computation.6 | loop fusion | flops 62902272 | bytes 50692096 | tf_op jit(solution)/shard_map/reduce_sum | solution.py:206
  377.0 20.7 %all_gather.53 = bf16[3,16,1024]{2,1,0:T(8,128)(2,1)S(1)} all-gather(bf16[3,16,256]{2,1,0:T(8,128)(2,1)S(1)} %get-tuple-element.102), channel_id=1, replica_groups=mesh['dp'=8,'blk'=4] {'blk'}, dimensions={2}, use_global_device_ids=true | all-gather | bytes 122880 | tf_op jit(solution)/shard_map/all_gather | solution.py:254
  397.7 50.5 %all-gather.14.cloned.1.call-done = bf16[3,1024,1024]{1,2,0:T(8,128)(2,1)} async-done(((bf16[3,256,1024]{1,2,0:T(8,128)(2,1)}), bf16[3,1024,1024]{1,2,0:T(8,128)(2,1)}) %all-gather.14.cloned.1.call-update) | async-done | bytes 6291472 | tf_op jit(solution)/shard_map/all_gather | solution.py:194
  448.2 23.8 %multiply_reduce_fusion = (f32[3,256,16]{1,2,0:T(8,128)S(1)}, bf16[3,256,16,64]{1,3,2,0:T(8,128)(2,1)}) fusion(bf16[3,256,16,64]{1,3,2,0:T(8,128)(2,1)S(1)} %copy-done.37, f32[3,256,16]{1,2,0:T(8,128)S(1)} %bitcast.204, bf16[3,1024,16,64]{1,3,2,0:T(8,128)(2,1)} %bitcast.220, f32[3,16,256,1024]{3,2,1,0:T(8,128)} %get-tuple-element.141, ...), kind=kOutput, calls=%fused_computation.86 | convolution fusion | flops 1677447168 | bytes 60178432 | tf_op jit(solution)/shard_map/shqk,skhe->sqhe/dot_general | solution.py:207
  472.0 28.8 %multiply_bitcast_fusion.1 = f32[3,256,16,64]{1,3,2,0:T(8,128)} fusion(bf16[3,1024,16,64]{1,3,2,0:T(8,128)(2,1)} %bitcast.175, f32[3,16,256,1024]{3,2,1,0:T(8,128)} %get-tuple-element.141, bf16[3,256,16,64]{1,3,2,0:T(8,128)(2,1)S(1)} %copy-done.37, bf16[3,1024,16,64]{1,3,2,0:T(8,128)(2,1)} %bitcast.221, f32[3,16,256]{2,1,0:T(8,128)S(1)} %bitcast.213, ...), kind=kOutput, calls=%fused_computation.85 | convolution fusion | flops 3297509376 | bytes 67993600 | tf_op jit(solution)/shard_map/shqk,skhe->sqhe/dot_general | solution.py:251
  500.8 27.4 %all_gather.55 = bf16[3,16,1024]{2,1,0:T(8,128)(2,1)S(1)} all-gather(bf16[3,16,256]{2,1,0:T(8,128)(2,1)S(1)} %bitcast_convert_fusion), channel_id=1, replica_groups=mesh['dp'=8,'blk'=4] {'blk'}, dimensions={2}, use_global_device_ids=true | all-gather | bytes 122880 | tf_op jit(solution)/shard_map/all_gather | solution.py:257
  528.9 35.5 %all-gather.22.cloned.1.call-done = bf16[3,1024,1024]{1,2,0:T(8,128)(2,1)} async-done(((bf16[3,256,1024]{1,2,0:T(8,128)(2,1)}), bf16[3,1024,1024]{1,2,0:T(8,128)(2,1)}) %all-gather.22.cloned.1.call-update) | async-done | bytes 6291472 | tf_op jit(solution)/shard_map/all_gather | solution.py:259
  564.4 22.0 %fusion.134 = f32[3,16,1024,256]{3,2,1,0:T(8,128)} fusion(bf16[3,1024,16,64]{1,3,2,0:T(8,128)(2,1)} %bitcast.179, bf16[3,256,16,48]{1,3,2,0:T(8,128)(2,1)S(1)} %copy-done.13, bf16[3,256,16,8]{1,3,2,0:T(8,128)(2,1)S(1)} %copy-done.34, bf16[3,256,16,8]{1,3,2,0:T(8,128)(2,1)S(1)} %copy-done.32), kind=kOutput, calls=%fused_computation.230 | convolution fusion | flops 1615331328 | bytes 58195968 | tf_op jit(solution)/shard_map/sqhe,skhe->shqk/dot_general | solution.py:265
  586.4 93.4 %all-gather.24.cloned.1.call-done = bf16[3,1024,1024]{2,1,0:T(8,128)(2,1)} async-done(((bf16[3,256,1024]{2,1,0:T(8,128)(2,1)}), bf16[3,1024,1024]{2,1,0:T(8,128)(2,1)}) %all-gather.24.cloned.1.call-update) | async-done | bytes 6291472 | tf_op jit(solution)/shard_map/all_gather | solution.py:260
  679.7 8.6 copy.80
  688.4 20.5 %fusion.64 = bf16[3,256,16,64]{1,3,2,0:T(8,128)(2,1)} fusion(bf16[3,1024,16,64]{1,3,2,0:T(8,128)(2,1)} %bitcast.191, f32[3,16,1024,256]{3,2,1,0:T(8,128)} %fusion.134, f32[3,16,1024]{2,1,0:T(8,128)S(1)} %convert_element_type.203, pred[1024,256]{1,0:T(8,128)(4,1)S(1)} %copy-done.63), kind=kOutput, calls=%fused_computation.97 | convolution fusion | flops 1661730816 | bytes 58654720 | tf_op jit(solution)/shard_map/shqk,sqhe->skhe/dot_general | solution.py:270
  708.9 27.8 %multiply_bitcast_fusion = f32[3,256,16,64]{1,3,2,0:T(8,128)} fusion(bf16[3,1024,16,64]{1,3,2,0:T(8,128)(2,1)} %bitcast.180, f32[3,16,1024,256]{3,2,1,0:T(8,128)} %fusion.134, bf16[3,1024,16,64]{1,3,2,0:T(8,128)(2,1)} %bitcast.192, bf16[3,256,16,64]{1,3,2,0:T(8,128)(2,1)} %bitcast.196, f32[3,16,1024]{2,1,0:T(8,128)} %convert_element_type.206, ...), kind=kOutput, calls=%fused_computation.83 | convolution fusion | flops 3297509376 | bytes 68288512 | tf_op jit(solution)/shard_map/shqk,sqhe->skhe/dot_general | solution.py:276
  767.9 12.3 fusion.135
  780.2 8.4 fusion.21
  788.6 262.7 %all-reduce.15.cloned.1.call-done = (f32[1024,384]{0,1:T(8,128)}, f32[4096,128]{1,0:T(8,128)}, f32[128,8192]{1,0:T(8,128)}, f32[128,1024]{1,0:T(8,128)}) async-done(((f32[1024,384]{0,1:T(8,128)}, f32[4096,128]{1,0:T(8,128)}, f32[128,8192]{1,0:T(8,128)}, f32[128,1024]{1,0:T(8,128)}), (f32[1024,384]{0,1:T(8,128)}, f32[4096,128]{1,0:T(8,128)}, f32[128,8192]{1,0:T(8,128)}, ...) | async-done | bytes 8388624 | tf_op jit(solution)/shard_map/psum | solution.py:299
  1054.9 13.5 %fusion.128 = (f32[1024]{0:T(1024)S(1)}, f32[768]{0:T(1024)S(1)}, f32[768]{0:T(1024)S(1)}, f32[1024]{0:T(1024)S(1)}, f32[768,1024]{1,0:T(8,128)S(1)}) fusion(f32[1024]{0:T(1024)S(1)} %bitcast.210, f32[768]{0:T(1024)S(1)} %copy-done.76, bf16[3,256,1024]{2,1,0:T(8,128)(2,1)S(1)} %copy-done.1, f32[768,1024]{1,0:T(8,128)S(1)} %convolution_add_fusion, ...), kind=kOutput, calls=%fused_computation.225 | convolution fusion | flops 6451097600 | bytes 25715712 | tf_op jit(solution)/shard_map/dot_general | solution.py:24
  1073.2 17.3 %all-reduce.8 = (f32[2,1024]{1,0:T(2,128)}, f32[2,1024]{1,0:T(2,128)}) all-reduce(f32[2,1024]{1,0:T(2,128)} %pad_maximum_fusion.2, f32[2,1024]{1,0:T(2,128)} %pad_maximum_fusion.3), channel_id=1, replica_groups=mesh['dp'=8,'blk'=4] {'blk'}, use_global_device_ids=true, to_apply=%region_12.13 | all-reduce | flops 4096 | bytes 32768 | tf_op jit(solution)/shard_map/psum | solution.py:299
  1090.5 24.1 %all-reduce.6 = (f32[2,1024]{1,0:T(2,128)}, f32[2,1024]{1,0:T(2,128)}) all-reduce(f32[2,1024]{1,0:T(2,128)} %get-tuple-element.88, f32[2,1024]{1,0:T(2,128)} %get-tuple-element.89), channel_id=1, replica_groups=mesh['dp'=8,'blk'=4] {'dp'}, use_global_device_ids=true, to_apply=%region_13.14 | all-reduce | flops 4096 | bytes 32768 | tf_op jit(solution)/shard_map/psum | solution.py:298
  1124.4 57.5 %all-reduce.13.cloned.1.call-done = (f32[1024,384]{0,1:T(8,128)}, f32[4096,128]{1,0:T(8,128)}, f32[128,8192]{1,0:T(8,128)}, f32[128,1024]{1,0:T(8,128)}) async-done(((f32[1024,384]{0,1:T(8,128)}, f32[4096,128]{1,0:T(8,128)}, f32[128,8192]{1,0:T(8,128)}, f32[128,1024]{1,0:T(8,128)}), (f32[1024,384]{0,1:T(8,128)}, f32[4096,128]{1,0:T(8,128)}, f32[128,8192]{1,0:T(8,128)}, ...) | async-done | bytes 8388624 | tf_op jit(solution)/shard_map/psum | solution.py:298
  1198.8 9.9 all_gather.57
  (352 shorter events, 161.8 us)
Async XLA Ops:
  7.2 95.3 %all-gather.10.cloned.1.call-start = ((), (), s32[]{:S(2)}) async-start(), calls=%async_computation | async-start | bytes 18874368 | tf_op jit(solution)/shard_map/all_gather | solution.py:161
  8.0 125.0 %all-gather.12.cloned.1.call-start = ((), (), s32[]{:S(2)}) async-start(), calls=%async_computation.1 | async-start | bytes 2359296 | tf_op jit(solution)/shard_map/all_gather | solution.py:165
  9.9 180.1 %all-gather.18.cloned.1.call-start = ((), (), s32[]{:S(2)}) async-start(), calls=%async_computation.4 | async-start | bytes 9437184 | tf_op jit(solution)/shard_map/all_gather | solution.py:162
  10.6 252.5 %all-gather.20.cloned.1.call-start = ((), (), s32[]{:S(2)}) async-start(), calls=%async_computation.5 | async-start | bytes 1179648 | tf_op jit(solution)/shard_map/all_gather | solution.py:164
  11.4 320.8 %all-gather.16.cloned.1.call-start = ((), (), s32[]{:S(2)}) async-start(), calls=%async_computation.3 | async-start | bytes 7864320 | tf_op jit(solution)/shard_map/all_gather | solution.py:193
  28.1 84.6 %copy-start.21 = (bf16[768,1024]{1,0:T(8,128)(2,1)}, bf16[768,1024]{1,0:T(8,128)(2,1)S(1)}, u32[]{:S(2)}) copy-start(bf16[768,1024]{1,0:T(8,128)(2,1)S(1)} %get-tuple-element.118) | copy-start | bytes 4718596
  29.9 103.1 %copy-start.43 = (bf16[768,128]{1,0:T(8,128)(2,1)}, bf16[768,128]{1,0:T(8,128)(2,1)S(1)}, u32[]{:S(2)}) copy-start(bf16[768,128]{1,0:T(8,128)(2,1)S(1)} %convolution_convert_fusion.3) | copy-start | bytes 589828
  30.0 121.3 %copy-start.71 = (f32[256,8]{0,1:T(8,128)}, f32[256,8]{0,1:T(8,128)S(1)}, u32[]{:S(2)}) copy-start(f32[256,8]{0,1:T(8,128)S(1)} %get-tuple-element.138) | copy-start | bytes 24580
  30.0 121.3 %copy-start.73 = (f32[256,8]{0,1:T(8,128)}, f32[256,8]{0,1:T(8,128)S(1)}, u32[]{:S(2)}) copy-start(f32[256,8]{0,1:T(8,128)S(1)} %get-tuple-element.139) | copy-start | bytes 24580
  154.7 293.5 %all-gather.14.cloned.1.call-start = ((), (), s32[]{:S(2)}) async-start(), calls=%async_computation.2 | async-start | bytes 7864320 | tf_op jit(solution)/shard_map/all_gather | solution.py:194
  158.5 405.9 %all-gather.22.cloned.1.call-start = ((), (), s32[]{:S(2)}) async-start(), calls=%async_computation.6 | async-start | bytes 7864320 | tf_op jit(solution)/shard_map/all_gather | solution.py:259
  175.7 112.7 %copy-start.6 = (bf16[768,1024]{1,0:T(8,128)(2,1)}, bf16[768,1024]{1,0:T(8,128)(2,1)S(1)}, u32[]{:S(2)}) copy-start(bf16[768,1024]{1,0:T(8,128)(2,1)S(1)} %fusion.28) | copy-start | bytes 4718596
  221.5 458.2 %all-gather.24.cloned.1.call-start = ((), (), s32[]{:S(2)}) async-start(), calls=%async_computation.7 | async-start | bytes 7864320 | tf_op jit(solution)/shard_map/all_gather | solution.py:260
  292.0 40.1 %copy-start.5 = (pred[256,1024]{1,0:T(8,128)(4,1)S(1)}, pred[256,1024]{1,0:T(8,128)(4,1)}, u32[]{:S(2)}) copy-start(pred[256,1024]{1,0:T(8,128)(4,1)} %iota_compare_fusion.1) | copy-start | bytes 786436
  292.1 40.1 %copy-start.14 = (bf16[3,256,16,48]{1,3,2,0:T(8,128)(2,1)S(1)}, bf16[3,256,16,48]{1,3,2,0:T(8,128)(2,1)}, u32[]{:S(2)}) copy-start(bf16[3,256,16,48]{1,3,2,0:T(8,128)(2,1)} %slice.131) | copy-start | bytes 3538948
  295.3 756.1 %all-reduce.15.cloned.1.call-start = ((), (), s32[]{:S(2)}) async-start(), calls=%async_computation.10 | async-start | bytes 16777216 | tf_op jit(solution)/shard_map/psum | solution.py:299
  354.0 94.2 %copy-start.37 = (bf16[3,256,16,64]{1,3,2,0:T(8,128)(2,1)S(1)}, bf16[3,256,16,64]{1,3,2,0:T(8,128)(2,1)}, u32[]{:S(2)}) copy-start(bf16[3,256,16,64]{1,3,2,0:T(8,128)(2,1)} %copy.77) | copy-start | bytes 4718596
  397.7 290.7 %copy-start.69 = (f32[3,16,1024]{2,1,0:T(8,128)}, f32[3,16,1024]{2,1,0:T(8,128)S(1)}, u32[]{:S(2)}) copy-start(f32[3,16,1024]{2,1,0:T(8,128)S(1)} %convert_element_type.203) | copy-start | bytes 589828
  500.8 63.6 %copy-start.13 = (bf16[3,256,16,48]{1,3,2,0:T(8,128)(2,1)S(1)}, bf16[3,256,16,48]{1,3,2,0:T(8,128)(2,1)}, u32[]{:S(2)}) copy-start(bf16[3,256,16,48]{1,3,2,0:T(8,128)(2,1)} %copy-done.12) | copy-start | bytes 3538948
  500.8 63.6 %copy-start.32 = (bf16[3,256,16,8]{1,3,2,0:T(8,128)(2,1)S(1)}, bf16[3,256,16,8]{1,3,2,0:T(8,128)(2,1)}, u32[]{:S(2)}) copy-start(bf16[3,256,16,8]{1,3,2,0:T(8,128)(2,1)} %copy-done.31) | copy-start | bytes 589828
  500.8 63.6 %copy-start.34 = (bf16[3,256,16,8]{1,3,2,0:T(8,128)(2,1)S(1)}, bf16[3,256,16,8]{1,3,2,0:T(8,128)(2,1)}, u32[]{:S(2)}) copy-start(bf16[3,256,16,8]{1,3,2,0:T(8,128)(2,1)} %copy-done.33) | copy-start | bytes 589828
  586.4 102.0 %copy-start.63 = (pred[1024,256]{1,0:T(8,128)(4,1)S(1)}, pred[1024,256]{1,0:T(8,128)(4,1)}, u32[]{:S(2)}) copy-start(pred[1024,256]{1,0:T(8,128)(4,1)} %iota_compare_fusion) | copy-start | bytes 786436
  708.9 27.8 %copy-start.72 = (f32[256,8]{0,1:T(8,128)S(1)}, f32[256,8]{0,1:T(8,128)}, u32[]{:S(2)}) copy-start(f32[256,8]{0,1:T(8,128)} %copy-done.71) | copy-start | bytes 24580
  708.9 27.8 %copy-start.74 = (f32[256,8]{0,1:T(8,128)S(1)}, f32[256,8]{0,1:T(8,128)}, u32[]{:S(2)}) copy-start(f32[256,8]{0,1:T(8,128)} %copy-done.73) | copy-start | bytes 24580
  760.1 421.8 %all-reduce.13.cloned.1.call-start = ((), (), s32[]{:S(2)}) async-start(), calls=%async_computation.9 | async-start | bytes 16777216 | tf_op jit(solution)/shard_map/psum | solution.py:298
  1051.4 166.8 %all-gather.26.cloned.1.call-start = ((), (), s32[]{:S(2)}) async-start(), calls=%async_computation.8 | async-start | bytes 2359296 | tf_op jit(solution)/shard_map/all_gather | solution.py:322
  1124.4 60.1 %copy-start.94 = (f32[768]{0:T(1024)S(1)}, f32[768]{0:T(1024)}, u32[]{:S(2)}) copy-start(f32[768]{0:T(1024)} %get-tuple-element.73) | copy-start | bytes 9220
  1124.4 60.1 %copy-start.39 = (bf16[128,1024]{1,0:T(8,128)(2,1)S(1)}, bf16[128,1024]{1,0:T(8,128)(2,1)}, u32[]{:S(2)}) copy-start(bf16[128,1024]{1,0:T(8,128)(2,1)} %copy-done.38) | copy-start | bytes 786436
  1124.4 60.1 %copy-start.56 = (bf16[768,128]{1,0:T(8,128)(2,1)S(1)}, bf16[768,128]{1,0:T(8,128)(2,1)}, u32[]{:S(2)}) copy-start(bf16[768,128]{1,0:T(8,128)(2,1)} %copy-done.55) | copy-start | bytes 589828
  1124.4 60.2 %copy-start.92 = (f32[1024]{0:T(1024)S(1)}, f32[1024]{0:T(1024)}, u32[]{:S(2)}) copy-start(f32[1024]{0:T(1024)} %convert_element_type.191) | copy-start | bytes 12292
  1124.4 60.2 %copy-start.93 = (f32[1024]{0:T(1024)S(1)}, f32[1024]{0:T(1024)}, u32[]{:S(2)}) copy-start(f32[1024]{0:T(1024)} %slice_convert_fusion.2) | copy-start | bytes 12292
  1184.5 29.3 %copy-start.30 = (f32[128,1024]{1,0:T(8,128)}, f32[128,1024]{1,0:T(8,128)S(1)}, u32[]{:S(2)}) copy-start(f32[128,1024]{1,0:T(8,128)S(1)} %get-tuple-element.99) | copy-start | bytes 1572868
  (87 other events, 621.9 us)
Sparse Core Ops, SparseCore 0:
  9.9 92.5 all-gather.9
  105.0 27.8 all-gather.11
  134.8 55.0 all-gather.17
  192.3 23.5 all-gather.19
  217.3 114.8 all-gather.15
  333.5 114.6 all-gather.13
  449.8 114.6 all-gather.21
  566.0 113.7 all-gather.23
  760.2 291.0 all-reduce.14
  1055.2 126.6 all-reduce.12
  1184.7 28.4 all-gather.25
